TPU v7x, 128 devices: a whole 4x4x4 slice. The times are simulated.
128 devices in a mesh: seq: 16 (over z_lo, x, core), res: 8 (over y, z_hi).
Axes of the slice: x: 4, y: 4, z: 4 (z_hi: 2, z_lo: 2; z = z_hi * 2 + z_lo), core: 2. Of those that a mesh axis runs over, the one named last changes fastest.
Arguments:
- states: bfloat16 [512, 256, 768], P('seq', 'res'), may hold values from -6 to 6
- row_query: bfloat16 [768, 768], replicated, as said below
- row_key: bfloat16 [768, 768], replicated
- row_value: bfloat16 [768, 768], replicated, may hold values from -0.21875 to 0.21875
- row_out: bfloat16 [768, 768], replicated, may hold values from -0.21875 to 0.21875
- col_query: bfloat16 [768, 768], replicated, as said below
- col_key: bfloat16 [768, 768], replicated
- col_value: bfloat16 [768, 768], replicated, may hold values from -0.21875 to 0.21875
- col_out: bfloat16 [768, 768], replicated, may hold values from -0.21875 to 0.21875
Outputs:
- updated: bfloat16 [512, 256, 768], P('seq', 'res')
Inputs may be any that keep to these rules, and one draw needn't show every extreme that they name: No bound on the size of row_query and row_key entries or of the scores they give is promised. No bound on the size of col_query and col_key entries or of the scores they give is promised.
All inputs are finite; a program needn't handle non-finite values.
Results may differ from a plain program's by a relative error of at most 0.02.
Values may be sent and summed in bfloat16 or wider, within the bound.
A program may use at most 128 MiB of HBM per device.

v0:
```python
import math
import jax
import jax.numpy as jnp
from jax import lax
from jax.sharding import PartitionSpec as P

D = 768
HEADS = 12
HD = D // HEADS


def normalize(states):
    values = states.astype(jnp.float32)
    center = values - jnp.mean(values, axis=-1, keepdims=True)
    spread = jnp.mean(center * center, axis=-1, keepdims=True)
    return (center * lax.rsqrt(spread + 1e-05)).astype(jnp.bfloat16)


def project(inputs, weight):
    return jnp.dot(inputs, weight, preferred_element_type=jnp.float32)


def on_device(
    states, row_query, row_key, row_value, row_out, col_query, col_key, col_value, col_out
):
    rows, cols = (states.shape[0], states.shape[1])
    seq, res = (lax.axis_size("seq"), lax.axis_size("res"))
    own_rows, own_cols = (rows // res, cols // seq)
    all_rows, all_cols = (rows * seq, cols * res)
    tied_scale = HD ** (-0.5) / math.sqrt(all_rows)
    moved = lax.all_to_all(
        states.reshape(res, own_rows, cols, D), "res", split_axis=0, concat_axis=0
    )
    by_row = moved.transpose(1, 0, 2, 3).reshape(own_rows, all_cols, D)
    normed = normalize(by_row)
    q1 = project(normed, row_query).astype(jnp.bfloat16).reshape(own_rows, all_cols, HEADS, HD)
    k1 = project(normed, row_key).astype(jnp.bfloat16).reshape(own_rows, all_cols, HEADS, HD)
    v1 = project(normed, row_value).astype(jnp.bfloat16).reshape(own_rows, all_cols, HEADS, HD)
    part = jnp.einsum("rihd,rjhd->hij", q1, k1, preferred_element_type=jnp.float32) * tied_scale
    part = part.reshape(HEADS * all_cols, all_cols)
    tied = lax.psum_scatter(part, ("seq", "res"), scatter_dimension=0, tiled=True)
    prob1 = jax.nn.softmax(tied, axis=-1).astype(jnp.bfloat16)
    prob1 = lax.all_gather(prob1, ("seq", "res"), axis=0, tiled=True)
    prob1 = prob1.reshape(HEADS, all_cols, all_cols)
    o1 = jnp.einsum("hij,rjhd->rihd", prob1, v1, preferred_element_type=jnp.float32)
    o1 = o1.astype(jnp.bfloat16).reshape(own_rows, all_cols, D)
    mid = (by_row.astype(jnp.float32) + project(o1, row_out)).astype(jnp.bfloat16)
    mid = mid.reshape(own_rows, res, seq, own_cols, D).transpose(2, 1, 0, 3, 4)
    mid = mid.reshape(seq * res, own_rows, own_cols, D)
    mid = lax.all_to_all(mid, ("seq", "res"), split_axis=0, concat_axis=0)
    mid = mid.reshape(all_rows, own_cols, D).transpose(1, 0, 2)
    normed2 = normalize(mid)
    q2 = project(normed2, col_query).astype(jnp.bfloat16).reshape(own_cols, all_rows, HEADS, HD)
    k2 = project(normed2, col_key).astype(jnp.bfloat16).reshape(own_cols, all_rows, HEADS, HD)
    v2 = project(normed2, col_value).astype(jnp.bfloat16).reshape(own_cols, all_rows, HEADS, HD)
    score = jnp.einsum("crhd,cshd->chrs", q2, k2, preferred_element_type=jnp.float32)
    prob2 = jax.nn.softmax(score * HD ** (-0.5), axis=-1).astype(jnp.bfloat16)
    o2 = jnp.einsum("chrs,cshd->crhd", prob2, v2, preferred_element_type=jnp.float32)
    o2 = o2.astype(jnp.bfloat16).reshape(own_cols, all_rows, D)
    colupd = project(o2, col_out).astype(jnp.bfloat16)
    updated = (mid.astype(jnp.float32) + colupd.astype(jnp.float32)).astype(jnp.bfloat16)
    updated = updated.reshape(own_cols, seq, rows, D).transpose(1, 2, 0, 3)
    updated = lax.all_to_all(updated, "seq", split_axis=0, concat_axis=0)
    return updated.transpose(1, 0, 2, 3).reshape(rows, cols, D)


def solution(mesh):
    placed = (P("seq", "res", None), P(), P(), P(), P(), P(), P(), P(), P())
    return jax.shard_map(
        on_device, mesh=mesh, in_specs=placed, out_specs=P("seq", "res", None), check_vma=False
    )
```

profile of v0, /device:TPU:1, one launch (start us, length us, event | category | flops | bytes accessed | tf_op | source)
XLA Modules:
  0.0 1114.7 jit_solution(17327529294043333661)
XLA Ops:
  6.5 29.4 %all_to_all.15 = bf16[8,4,32,768]{3,2,1,0:T(8,128)(2,1)S(1)} all-to-all(bf16[8,4,32,768]{3,2,1,0:T(8,128)(2,1)} %bitcast.110), channel_id=1, replica_groups=mesh['seq'=16,'res'=8] {'res'}, dimensions={0} | all-to-all | bytes 3145728 | tf_op jit(solution)/shard_map/all_to_all | solution.py:31
  35.9 0.3 fusion.13
  36.2 0.1 div.31
  36.3 0.6 multiply_reduce_fusion.2
  37.0 0.4 convert_bitcast_fusion
  37.4 0.3 copy.94
  37.7 0.4 fusion.10
  38.1 1.3 copy-done.2
  39.4 1.1 copy-done.4
  40.5 1.4 convolution_convert_fusion.5
  41.9 0.7 copy.100
  42.6 4.3 convolution_convert_fusion.6
  46.9 1.7 copy.99
  48.6 2.3 bitcast_multiply_fusion
  51.0 0.2 all-gather.2.cloned.1.call-start
  51.2 633.3 %reduce-scatter.2.cloned.1.call-done = f32[24,256]{1,0:T(8,128)} async-done(((f32[3072,256]{1,0:T(8,128)}), f32[24,256]{1,0:T(8,128)}) %reduce-scatter.2.cloned.1.call-update) | async-done | bytes 24592 | tf_op jit(solution)/shard_map/reduce_scatter | solution.py:41
  684.5 0.8 reduce_max.18
  685.4 0.9 fusion.26
  686.3 1.4 divide_convert_fusion.4
  687.8 2.7 convolution_convert_fusion.7
  690.4 0.7 copy.98
  691.1 299.8 %all-gather.2.cloned.1.call-done = bf16[3072,256]{1,0:T(8,128)(2,1)} async-done(((bf16[24,256]{1,0:T(8,128)(2,1)}), bf16[3072,256]{1,0:T(8,128)(2,1)}) %all-gather.2.cloned.1.call-update) | async-done | bytes 1572880 | tf_op jit(solution)/shard_map/all_gather | solution.py:43
  990.9 2.1 fusion.15
  993.1 0.2 copy.102
  993.2 1.7 copy-done.3
  994.9 1.5 fusion.11
  996.5 0.6 reshape.103
  997.1 0.9 copy.138
  998.0 1.6 copy.105
  999.6 31.3 %all_to_all.16 = bf16[128,4,2,768]{3,2,1,0:T(2,128)(2,1)S(1)} all-to-all(bf16[128,4,2,768]{3,2,1,0:T(2,128)(2,1)S(1)} %copy.105), channel_id=1, replica_groups=mesh['seq'=16,'res'=8] {'seq','res'}, dimensions={0} | all-to-all | bytes 3145728 | tf_op jit(solution)/shard_map/all_to_all | solution.py:50
  1030.9 0.3 copy_convert_fusion
  1031.2 2.4 copy.107
  1033.6 0.3 bitcast_reduce_fusion
  1033.9 0.5 multiply_reduce_fusion.1
  1034.4 0.4 multiply_convert_fusion
  1034.8 1.1 copy-done.6
  1035.9 2.6 convolution_convert_fusion.1
  1038.5 2.6 copy.111
  1041.1 4.4 convolution_convert_fusion.2
  1045.5 2.5 convolution_convert_fusion.3
  1048.1 2.6 copy.109
  1050.7 2.6 copy.110
  1053.3 14.2 %fusion.30 = (f32[2,12,512]{2,1,0:T(8,128)S(1)}, f32[2,12,512,512]{2,3,1,0:T(8,128)}) fusion(bf16[2,512,12,64]{1,3,2,0:T(8,128)(2,1)} %bitcast.113, bf16[2,512,12,64]{1,3,2,0:T(8,128)(2,1)} %bitcast.111), kind=kOutput, calls=%fused_computation.55 | convolution fusion | flops 824181248 | bytes 28360704 | tf_op jit(solution)/shard_map/sub | solution.py:57
  1067.5 11.0 fusion.12
  1078.5 1.4 fusion.8
  1079.9 0.1 copy.137
  1080.1 25.8 %all_to_all.17 = bf16[16,32,2,768]{3,1,2,0:T(8,128)(2,1)S(1)} all-to-all(bf16[16,32,2,768]{3,1,2,0:T(8,128)(2,1)S(1)} %bitcast.105), channel_id=1, replica_groups=mesh['seq'=16,'res'=8] {'seq'}, dimensions={0} | all-to-all | bytes 3145728 | tf_op jit(solution)/shard_map/all_to_all | solution.py:63
  1105.9 2.0 copy.115
  (29 shorter events, 0.2 us)
Async XLA Ops:
  6.5 34.0 %copy-start = (bf16[768,768]{1,0:T(8,128)(2,1)S(1)}, bf16[768,768]{1,0:T(8,128)(2,1)}, u32[]{:S(2)}) copy-start(bf16[768,768]{1,0:T(8,128)(2,1)} %param.11) | copy-start | bytes 3538948
  6.5 678.0 %reduce-scatter.2.cloned.1.call-start = ((), (), s32[]{:S(2)}) async-start(), calls=%async_computation.4 | async-start | bytes 3170304 | tf_op jit(solution)/shard_map/reduce_scatter | solution.py:41
  37.7 1.7 copy-start.2
  39.4 1.1 copy-start.4
  50.9 636.8 %copy-start.5 = (bf16[4,256,768]{2,1,0:T(8,128)(2,1)S(1)}, bf16[4,256,768]{2,1,0:T(8,128)(2,1)}, u32[]{:S(2)}) copy-start(bf16[4,256,768]{2,1,0:T(8,128)(2,1)} %copy-done.4) | copy-start | bytes 4718596
  51.0 940.0 %all-gather.2.cloned.1.call-start = ((), (), s32[]{:S(2)}) async-start(), calls=%async_computation.5 | async-start | bytes 1585152 | tf_op jit(solution)/shard_map/all_gather | solution.py:43
  990.9 2.3 copy-start.8
  993.0 1.9 copy-start.3
  1034.4 1.5 copy-start.9
  1034.7 1.1 copy-start.6
  1041.1 4.4 copy-start.7
  1041.1 4.4 copy-start.10
  1067.5 11.0 copy-start.11
  1105.9 2.0 copy-start.1
Sparse Core Ops, SparseCore 0:
  51.1 633.3 reduce-scatter.1
  687.9 303.0 all-gather.1
where the time goes:
time: 1120 us; the launch traced here: 1110 us
  waiting for transfers between devices  933 us (83%)
  blocking collectives  86.4 us (8%)
  matrix products  50.5 us (5%)
  local copies, waits for them, and re-layouts  24.6 us (2%)
  between operations  13.6 us (1%)
    reduce_scatter x1, waiting for transfers between devices, on_device(): lax.psum_scatter(part, ('seq', 'res'), scatter_dimension=0, tiled=True)  633 us
    all_gather x1, waiting for transfers between devices, on_device(): prob1 = lax.all_gather(prob1, ('seq', 'res'), axis=0, tiled=True)  300 us
    all_to_all x1, blocking collectives, on_device(): mid = lax.all_to_all(mid, ('seq', 'res'), split_axis=0, concat_axis=0)  31.3 us
    all_to_all x1, blocking collectives, on_device(): lax.all_to_all(states.reshape(res, own_rows, cols, D), 'res', split_axis=...  29.4 us
    all_to_all x1, blocking collectives, on_device(): updated = lax.all_to_all(updated, 'seq', split_axis=0, concat_axis=0)  25.8 us
  transfers between devices with their start and end apart: 2, of which 2 were waited for; matrix products, arithmetic and copies ran while one was open for 0% of the time, Pallas kernels for 0%

commit v1 on v0

--- a/solution.py
+++ b/solution.py
@@ -40,7 +40,10 @@
     part = part.reshape(HEADS * all_cols, all_cols)
     tied = lax.psum_scatter(part, ("seq", "res"), scatter_dimension=0, tiled=True)
     prob1 = jax.nn.softmax(tied, axis=-1).astype(jnp.bfloat16)
-    prob1 = lax.all_gather(prob1, ("seq", "res"), axis=0, tiled=True)
+    prob1 = jnp.concatenate(
+        lax.all_to_all(jnp.stack([prob1] * lax.axis_size(("seq", "res"))), ("seq", "res"), 0, 0),
+        axis=0,
+    )
     prob1 = prob1.reshape(HEADS, all_cols, all_cols)
     o1 = jnp.einsum("hij,rjhd->rihd", prob1, v1, preferred_element_type=jnp.float32)
     o1 = o1.astype(jnp.bfloat16).reshape(own_rows, all_cols, D)

time: 1120 us -> 846 us (0.76)
  waiting for transfers between devices: 933 us -> 652 us
  starting transfers between devices: 0.22 us -> 13.8 us
    all_gather x1 -> x0, waiting for transfers between devices: 300 us -> none  [on_device(): prob1 = lax.all_gather(prob1, ('seq', 'res'), axis=0, tiled=True)]
    all_to_all x0 -> x1, waiting for transfers between devices: none -> 18 us  [on_device(): lax.all_to_all(jnp.stack([prob1] * lax.axis_size(('seq', 'res'))), ('seq'...]
    all_to_all x0 -> x1, starting transfers between devices: none -> 13.8 us  [on_device(): lax.all_to_all(jnp.stack([prob1] * lax.axis_size(('seq', 'res'))), ('seq'...]
  transfers between devices with their start and end apart: 2 -> 2, of which waited for: 2 -> 2; matrix products, arithmetic and copies ran while one was open for 0% -> 1% of each run, Pallas kernels for 0% -> 0%
where the time goes in v1:
time: 846 us
  waiting for transfers between devices  652 us (77%)
  blocking collectives  83.9 us (10%)
  matrix products  50.1 us (6%)
  local copies, waits for them, and re-layouts  26.9 us (3%)
  starting transfers between devices  13.8 us (2%)
  between operations  13.6 us (2%)
    reduce_scatter x1, waiting for transfers between devices, on_device(): lax.psum_scatter(part, ('seq', 'res'), scatter_dimension=0, tiled=True)  634 us
    all_to_all x1, blocking collectives, on_device(): lax.all_to_all(states.reshape(res, own_rows, cols, D), 'res', split_axis=...  29.4 us
    all_to_all x1, blocking collectives, on_device(): mid = lax.all_to_all(mid, ('seq', 'res'), split_axis=0, concat_axis=0)  28.7 us
    all_to_all x1, blocking collectives, on_device(): updated = lax.all_to_all(updated, 'seq', split_axis=0, concat_axis=0)  25.8 us
    dot_general x8, matrix products, project(): return jnp.dot(inputs, weight, preferred_element_type=jnp.float32)  22 us
    all_to_all x1, waiting for transfers between devices, on_device(): lax.all_to_all(jnp.stack([prob1] * lax.axis_size(('seq', 'res'))), ('seq'...  18 us
  transfers between devices with their start and end apart: 2, of which 2 were waited for; matrix products, arithmetic and copies ran while one was open for 1% of the time, Pallas kernels for 0%

profile of v1, /device:TPU:1, one launch (start us, length us, event | category | flops | bytes accessed | tf_op | source)
XLA Modules:
  0.0 845.6 jit_solution(3438349429834159391)
XLA Ops:
  6.5 29.4 %all_to_all.20 = bf16[8,4,32,768]{3,2,1,0:T(8,128)(2,1)S(1)} all-to-all(bf16[8,4,32,768]{3,2,1,0:T(8,128)(2,1)} %bitcast.111), channel_id=1, replica_groups=mesh['seq'=16,'res'=8] {'res'}, dimensions={0} | all-to-all | bytes 3145728 | tf_op jit(solution)/shard_map/all_to_all | solution.py:31
  35.9 0.3 fusion.13
  36.3 0.6 multiply_reduce_fusion.2
  37.0 0.4 convert_bitcast_fusion
  37.4 0.3 copy.94
  37.7 0.4 fusion.10
  38.1 1.3 copy-done.2
  39.4 1.1 copy-done.4
  40.5 1.4 convolution_convert_fusion.5
  41.9 0.7 copy.100
  42.6 4.3 convolution_convert_fusion.6
  46.9 1.7 copy.99
  48.6 2.3 bitcast_multiply_fusion
  51.0 633.6 %reduce-scatter.2.cloned.1.call-done = f32[24,256]{1,0:T(8,128)} async-done(((f32[3072,256]{1,0:T(8,128)}), f32[24,256]{1,0:T(8,128)}) %reduce-scatter.2.cloned.1.call-update) | async-done | bytes 24592 | tf_op jit(solution)/shard_map/reduce_scatter | solution.py:41
  684.5 0.8 reduce_max.18
  685.4 0.9 fusion.26
  686.3 0.8 divide_convert_fusion.4
  687.1 1.2 stack.2
  688.4 13.8 %all-to-all-start.1 = ((bf16[128,24,256]{2,1,0:T(8,128)(2,1)}), bf16[128,24,256]{2,1,0:T(8,128)(2,1)S(1)}, u32[]{:S(2)}, u32[]{:S(2)}) async-start(bf16[128,24,256]{2,1,0:T(8,128)(2,1)} %stack.2), calls=%async_computation.2 | async-start | bytes 3145728 | tf_op jit(solution)/shard_map/all_to_all | solution.py:44
  702.2 3.8 convolution_convert_fusion.7
  706.0 1.7 copy.98
  707.8 18.0 %all-to-all-done.1 = bf16[128,24,256]{2,1,0:T(8,128)(2,1)S(1)} async-done(((bf16[128,24,256]{2,1,0:T(8,128)(2,1)}), bf16[128,24,256]{2,1,0:T(8,128)(2,1)S(1)}, u32[]{:S(2)}, u32[]{:S(2)}) %all-to-all-start.1) | async-done | bytes 1572896 | tf_op jit(solution)/shard_map/all_to_all | solution.py:44
  725.7 0.6 fusion.15
  726.3 0.2 copy.102
  726.5 0.5 copy-done.8
  727.0 1.3 copy-done.3
  728.3 1.5 fusion.11
  729.8 0.6 reshape.101
  730.5 0.9 copy.138
  731.3 1.6 copy.105
  733.0 28.7 %all_to_all.21 = bf16[128,4,2,768]{3,2,1,0:T(2,128)(2,1)S(1)} all-to-all(bf16[128,4,2,768]{3,2,1,0:T(2,128)(2,1)S(1)} %copy.105), channel_id=1, replica_groups=mesh['seq'=16,'res'=8] {'seq','res'}, dimensions={0} | all-to-all | bytes 3145728 | tf_op jit(solution)/shard_map/all_to_all | solution.py:53
  761.7 0.3 copy_convert_fusion
  762.0 2.4 copy.107
  764.4 0.3 bitcast_reduce_fusion
  764.7 0.5 multiply_reduce_fusion.1
  765.2 0.4 multiply_convert_fusion
  765.6 1.1 copy-done.6
  766.7 2.6 convolution_convert_fusion.1
  769.3 2.6 copy.111
  771.9 4.4 convolution_convert_fusion.2
  776.4 2.5 convolution_convert_fusion.3
  778.9 2.6 copy.109
  781.5 2.6 copy.110
  784.1 14.2 %fusion.30 = (f32[2,12,512]{2,1,0:T(8,128)S(1)}, f32[2,12,512,512]{2,3,1,0:T(8,128)}) fusion(bf16[2,512,12,64]{1,3,2,0:T(8,128)(2,1)} %bitcast.114, bf16[2,512,12,64]{1,3,2,0:T(8,128)(2,1)} %bitcast.112), kind=kOutput, calls=%fused_computation.55 | convolution fusion | flops 824181248 | bytes 28360704 | tf_op jit(solution)/shard_map/sub | solution.py:60
  798.3 11.0 %fusion.12 = bf16[2,12,64,512]{3,2,1,0:T(8,128)(2,1)S(1)} fusion(bf16[2,512,12,64]{1,3,2,0:T(8,128)(2,1)} %bitcast.113, f32[2,12,512,512]{2,3,1,0:T(8,128)} %get-tuple-element.6, f32[2,12,512]{2,1,0:T(8,128)S(1)} %get-tuple-element.5), kind=kOutput, calls=%fused_computation.22 | convolution fusion | flops 818675712 | bytes 28360704 | tf_op jit(solution)/shard_map/chrs,cshd->crhd/dot_general | solution.py:61
  809.3 1.4 fusion.8
  810.9 25.8 %all_to_all.22 = bf16[16,32,2,768]{3,1,2,0:T(8,128)(2,1)S(1)} all-to-all(bf16[16,32,2,768]{3,1,2,0:T(8,128)(2,1)S(1)} %bitcast.105), channel_id=1, replica_groups=mesh['seq'=16,'res'=8] {'seq'}, dimensions={0} | all-to-all | bytes 3145728 | tf_op jit(solution)/shard_map/all_to_all | solution.py:66
  836.7 2.0 copy.115
  (29 shorter events, 0.4 us)
Async XLA Ops:
  6.5 34.0 %copy-start = (bf16[768,768]{1,0:T(8,128)(2,1)S(1)}, bf16[768,768]{1,0:T(8,128)(2,1)}, u32[]{:S(2)}) copy-start(bf16[768,768]{1,0:T(8,128)(2,1)} %param.11) | copy-start | bytes 3538948
  6.5 678.0 %reduce-scatter.2.cloned.1.call-start = ((), (), s32[]{:S(2)}) async-start(), calls=%async_computation.5 | async-start | bytes 3170304 | tf_op jit(solution)/shard_map/reduce_scatter | solution.py:41
  37.7 1.7 copy-start.2
  39.4 1.1 copy-start.4
  688.4 13.9 %copy-start.5 = (bf16[4,256,768]{2,1,0:T(8,128)(2,1)S(1)}, bf16[4,256,768]{2,1,0:T(8,128)(2,1)}, u32[]{:S(2)}) copy-start(bf16[4,256,768]{2,1,0:T(8,128)(2,1)} %copy-done.4) | copy-start | bytes 4718596
  688.4 37.3 %all-to-all-start.1 = ((bf16[128,24,256]{2,1,0:T(8,128)(2,1)}), bf16[128,24,256]{2,1,0:T(8,128)(2,1)S(1)}, u32[]{:S(2)}, u32[]{:S(2)}) async-start(bf16[128,24,256]{2,1,0:T(8,128)(2,1)} %stack.2), calls=%async_computation.2 | async-start | bytes 3145728 | tf_op jit(solution)/shard_map/all_to_all | solution.py:44
  725.7 1.3 copy-start.8
  726.3 2.0 copy-start.3
  765.2 1.5 copy-start.9
  765.6 1.1 copy-start.6
  771.9 4.4 copy-start.7
  771.9 4.4 copy-start.10
  798.3 11.0 %copy-start.11 = (bf16[768,768]{1,0:T(8,128)(2,1)S(1)}, bf16[768,768]{1,0:T(8,128)(2,1)}, u32[]{:S(2)}) copy-start(bf16[768,768]{1,0:T(8,128)(2,1)} %param.17) | copy-start | bytes 3538948
  836.7 2.0 copy-start.1
Sparse Core Ops, SparseCore 0:
  51.1 633.3 reduce-scatter.1
